TPU v7x, 32 devices: a whole 2x2x4 slice. The times are simulated.
32 devices in a mesh: rows: 8 (over y, x, core), cols: 4 (over z).
Axes of the slice: x: 2, y: 2, z: 4, core: 2. Of those that a mesh axis runs over, the one named last changes fastest.
Arguments:
- white_real: float32 [4096, 4096], P('rows', 'cols'), may hold values from -6 to 6
- white_imag: float32 [4096, 4096], P('rows', 'cols'), may hold values from -6 to 6
- covariates: bfloat16 [16, 4096, 4096], P(None, 'rows', 'cols'), may hold values from -6 to 6
- coefficients: float32 [16], replicated, may hold values from -0.9 to 0.9
- counts: int32 [4096, 4096], P('rows', 'cols'), may hold values from 0 to 5
- land_mask: int32 [4096, 4096], P('rows', 'cols'), may hold values from 0 to 1
- field_hyper: float32 [2], replicated, may hold values from 1 to 2
Outputs:
- step_real: float32 [4096, 4096], P('rows', 'cols')
- step_imag: float32 [4096, 4096], P('rows', 'cols')
- coef_grad: float32 [16], replicated
- objective: float32 [], replicated
All inputs are finite; a program needn't handle non-finite values.
Results may differ from a plain program's by a relative error of at most 0.0003.
Values sent between devices are 32-bit elements; how exact they have to be, the bound alone decides.
No kernel may reach another device: no remote copies, remote signals or barrier semaphores. Data moves between devices by JAX's collectives and lax.ppermute only.
A program may use at most 128 MiB of HBM per device.

v0:
```python
import math
import jax
import jax.numpy as jnp
from jax import lax
from jax.sharding import PartitionSpec as P

NG = 4096
lasso_weight = 0.02
ridge_weight = 0.1


def field_spectrum(field_hyper, wave_row, wave_col):
    amplitude = 0.2 * field_hyper[0]
    freq_range = field_hyper[1]
    radius = (wave_row[:, None] * wave_row[:, None] + wave_col[None, :] * wave_col[None, :]) / (
        freq_range * freq_range
    )
    return amplitude * (1.0 + NG / freq_range * jnp.power(1.0 + radius, -0.75))


def angle_table(left_len, right_len, modulus):
    product = lax.iota(jnp.int32, left_len)[:, None] * lax.iota(jnp.int32, right_len)[None, :]
    angles = (product % modulus).astype(jnp.float32) * (2.0 * math.pi / modulus)
    return (jnp.cos(angles), jnp.sin(angles))


def inverse_transform(pieces, want_real):
    highest = lax.Precision.HIGHEST
    components = pieces.shape[0]
    row_count = pieces.shape[1]
    length = pieces.shape[2]
    factor = 8
    others = length // factor
    shaped = pieces.reshape(components, row_count, others, factor)
    big_cos, big_sin = angle_table(others, others, others)

    def apply_big(table, block):
        return jnp.einsum("rnm,nk->rmk", block, table, precision=highest)

    if components == 2:
        real_mid = apply_big(big_cos, shaped[0]) - apply_big(big_sin, shaped[1])
        imag_mid = apply_big(big_sin, shaped[0]) + apply_big(big_cos, shaped[1])
    else:
        real_mid = apply_big(big_cos, shaped[0])
        imag_mid = apply_big(big_sin, shaped[0])
    tw_cos, tw_sin = angle_table(factor, others, length)
    real_tw = real_mid * tw_cos - imag_mid * tw_sin
    imag_tw = real_mid * tw_sin + imag_mid * tw_cos
    small_cos, small_sin = angle_table(factor, factor, factor)

    def apply_small(table, block):
        return jnp.einsum("rmk,mj->rjk", block, table, precision=highest)

    real_out = (apply_small(small_cos, real_tw) - apply_small(small_sin, imag_tw)).reshape(
        1, row_count, length
    )
    if want_real:
        return real_out
    imag_out = (apply_small(small_sin, real_tw) + apply_small(small_cos, imag_tw)).reshape(
        1, row_count, length
    )
    return jnp.concatenate([real_out, imag_out], axis=0)


def middle_step(spread):
    returned = lax.all_to_all(spread, "cols", split_axis=2, concat_axis=1, tiled=True)
    flipped = jnp.swapaxes(returned, 1, 2)
    return lax.all_to_all(flipped, "rows", split_axis=1, concat_axis=2, tiled=True)


def grid_transform(pieces, want_real):
    full_rows = lax.all_to_all(pieces, "cols", split_axis=1, concat_axis=2, tiled=True)
    halfway = inverse_transform(full_rows, False)
    columns = middle_step(halfway)
    second = inverse_transform(columns, want_real)
    blocks_out = lax.all_to_all(second, "rows", split_axis=2, concat_axis=1, tiled=True)
    return jnp.swapaxes(blocks_out, 1, 2) * (1.0 / NG)


def shards(white_real, white_imag, covariates, coefficients, counts, land_mask, field_hyper):
    highest = lax.Precision.HIGHEST
    rows_here = white_real.shape[0]
    cols_here = white_real.shape[1]
    freq_row = lax.axis_index("rows") * rows_here + lax.iota(jnp.int32, rows_here)
    freq_col = lax.axis_index("cols") * cols_here + lax.iota(jnp.int32, cols_here)
    wave_row = jnp.minimum(freq_row, NG - freq_row).astype(jnp.float32)
    wave_col = jnp.minimum(freq_col, NG - freq_col).astype(jnp.float32)
    spectrum = field_spectrum(field_hyper, wave_row, wave_col)
    scaled = jnp.stack([spectrum * white_real, spectrum * white_imag])
    latent = grid_transform(scaled, True)[0]
    cov_full = covariates.astype(jnp.float32)
    linear = jnp.einsum("j,jrc->rc", coefficients, cov_full, precision=highest)
    log_rate = linear + latent
    intensity = jnp.exp(log_rate)
    land_vals = land_mask.astype(jnp.float32)
    count_vals = counts.astype(jnp.float32)
    residual = land_vals * (intensity - count_vals)
    partial_coef = jnp.einsum("jrc,rc->j", cov_full, residual, precision=highest)
    partial_loss = jnp.sum(land_vals * (intensity - count_vals * log_rate)) + 0.5 * jnp.sum(
        white_real * white_real + white_imag * white_imag
    )
    adjoint = grid_transform(residual[None], False)
    total_coef, total_loss = lax.psum((partial_coef, partial_loss), ("rows", "cols"))
    per_cell = 1.0 / (NG * NG)
    coef_grad = (
        total_coef * per_cell + lasso_weight * jnp.sign(coefficients) + ridge_weight * coefficients
    )
    objective = (
        total_loss * per_cell
        + lasso_weight * jnp.sum(jnp.abs(coefficients))
        + 0.5 * ridge_weight * jnp.sum(coefficients * coefficients)
    )
    curvature = 1.0 + spectrum * spectrum
    step_real = (spectrum * adjoint[0] + white_real) / curvature
    step_imag = (white_imag - spectrum * adjoint[1]) / curvature
    return (step_real, step_imag, coef_grad, objective)


def solution(mesh):
    return jax.shard_map(
        shards,
        mesh=mesh,
        in_specs=(
            P("rows", "cols"),
            P("rows", "cols"),
            P(None, "rows", "cols"),
            P(),
            P("rows", "cols"),
            P("rows", "cols"),
            P(),
        ),
        out_specs=(P("rows", "cols"), P("rows", "cols"), P(), P()),
        check_vma=False,
    )
```

profile of v0, /device:TPU:0, one launch (start us, length us, event | category | flops | bytes accessed | tf_op | source)
XLA Modules:
  0.0 896.9 jit_solution(2084490301962304620)
XLA Ops:
  24.5 93.3 %all-to-all-done = f32[2,512,1024]{2,0,1:T(2,128)} async-done(((f32[2,512,1024]{2,0,1:T(2,128)}), f32[2,512,1024]{2,0,1:T(2,128)}, u32[]{:S(2)}, u32[]{:S(2)}) %all-to-all-start) | async-done | bytes 4194336 | tf_op jit(solution)/shard_map/all_to_all | solution.py:72
  127.4 10.3 %fusion.62 = f32[128,8,512]{2,0,1:T(8,128)} fusion(f32[128,512,8]{1,0,2:T(8,128)} %copy.151), kind=kOutput, calls=%fused_computation.88 | convolution fusion | flops 3224895488 | bytes 4194304 | tf_op jit(solution)/shard_map/rnm,nk->rmk/dot_general | solution.py:38
  137.6 8.4 fusion.74
  149.8 9.9 %convolution_subtract_fusion.2 = f32[128,8,512]{2,0,1:T(8,128)S(1)} fusion(f32[128,8,512]{2,0,1:T(8,128)} %fusion.74, f32[128,512,8]{1,0,2:T(8,128)S(1)} %copy.153), kind=kOutput, calls=%fused_computation.73 | convolution fusion | flops 3225419776 | bytes 6291456 | tf_op jit(solution)/shard_map/rnm,nk->rmk/dot_general | solution.py:38
  159.8 9.2 %multiply_subtract_fusion.3 = (f32[128,8,512]{2,0,1:T(8,128)S(1)}, f32[128,8,512]{2,0,1:T(8,128)S(1)}) fusion(f32[128,8,512]{2,0,1:T(8,128)S(1)} %convolution_subtract_fusion.2, f32[8,512]{1,0:T(8,128)S(1)} %get-tuple-element.32, f32[8,512]{1,0:T(8,128)S(1)} %get-tuple-element.33, f32[128,8,512]{2,0,1:T(8,128)S(1)} %copy-done.8, f32[128,512,8]{1,0,2:T(8,128)S(1)} %copy.153), kind=kOutput, calls=%fused_computation.41 | convolution fusion | flops 3228565504 | bytes 10518528 | tf_op jit(solution)/shard_map/rnm,nk->rmk/dot_general | solution.py:38
  192.2 95.3 %all_to_all.114 = f32[2,128,4096]{1,0,2:T(2,128)S(1)} all-to-all(f32[2,128,4096]{1,0,2:T(2,128)S(1)} %pad_maximum_fusion.1), channel_id=1, replica_groups=mesh['rows'=8,'cols'=4] {'cols'}, dimensions={2} | all-to-all | bytes 8388608 | tf_op jit(solution)/shard_map/all_to_all | solution.py:66
  302.5 52.9 %all_to_all.115 = f32[2,1024,512]{2,0,1:T(2,128)S(1)} all-to-all(f32[2,1024,512]{2,0,1:T(2,128)} %copy.164), channel_id=1, replica_groups=mesh['rows'=8,'cols'=4] {'rows'}, dimensions={1} | all-to-all | bytes 8388608 | tf_op jit(solution)/shard_map/all_to_all | solution.py:68
  362.6 10.3 %fusion.59 = f32[128,8,512]{2,0,1:T(8,128)} fusion(f32[128,512,8]{1,0,2:T(8,128)} %copy.167), kind=kOutput, calls=%fused_computation.85 | convolution fusion | flops 3224895488 | bytes 4194304 | tf_op jit(solution)/shard_map/rnm,nk->rmk/dot_general | solution.py:38
  372.9 8.4 fusion.71
  385.0 9.9 %convolution_subtract_fusion.1 = f32[128,8,512]{2,0,1:T(8,128)S(1)} fusion(f32[128,8,512]{2,0,1:T(8,128)} %fusion.71, f32[128,512,8]{1,0,2:T(8,128)S(1)} %copy.169), kind=kOutput, calls=%fused_computation.71 | convolution fusion | flops 3225419776 | bytes 6291456 | tf_op jit(solution)/shard_map/rnm,nk->rmk/dot_general | solution.py:38
  395.0 9.2 %multiply_subtract_fusion.2 = (f32[128,8,512]{2,0,1:T(8,128)S(1)}, f32[128,8,512]{2,0,1:T(8,128)S(1)}) fusion(f32[128,8,512]{2,0,1:T(8,128)S(1)} %convolution_subtract_fusion.1, f32[8,512]{1,0:T(8,128)S(1)} %get-tuple-element.32, f32[8,512]{1,0:T(8,128)S(1)} %get-tuple-element.33, f32[128,8,512]{2,0,1:T(8,128)S(1)} %copy-done.9, f32[128,512,8]{1,0,2:T(8,128)S(1)} %copy.169), kind=kOutput, calls=%fused_computation.37 | convolution fusion | flops 3228565504 | bytes 10518528 | tf_op jit(solution)/shard_map/rnm,nk->rmk/dot_general | solution.py:38
  415.8 22.7 %fusion = f32[1,512,1024]{2,0,1:T(1,128)} fusion(bf16[16,512,1024]{2,1,0:T(8,128)(2,1)} %param.9, f32[16]{0:T(128)S(1)} %copy-done.18), kind=kOutput, calls=%fused_computation.1 | convolution fusion | flops 100663296 | bytes 18874432 | tf_op jit(solution)/shard_map/j,jrc->rc/dot_general | solution.py:92
  449.1 48.1 %all_to_all.116 = f32[1,512,1024]{2,0,1:T(1,128)S(1)} all-to-all(f32[1,512,1024]{2,0,1:T(1,128)S(1)} %broadcast_in_dim.2), channel_id=1, replica_groups=mesh['rows'=8,'cols'=4] {'cols'}, dimensions={1} | all-to-all | bytes 4194304 | tf_op jit(solution)/shard_map/all_to_all | solution.py:72
  501.4 8.4 fusion.68
  509.8 9.0 %multiply_subtract_fusion.1 = (f32[128,8,512]{2,0,1:T(8,128)S(1)}, f32[128,8,512]{2,0,1:T(8,128)S(1)}) fusion(f32[128,8,512]{2,0,1:T(8,128)S(1)} %fusion.68, f32[8,512]{1,0:T(8,128)S(1)} %get-tuple-element.32, f32[8,512]{1,0:T(8,128)S(1)} %get-tuple-element.33, f32[128,512,8]{1,0,2:T(8,128)S(1)} %copy.177), kind=kOutput, calls=%fused_computation.33 | convolution fusion | flops 3228041216 | bytes 8421376 | tf_op jit(solution)/shard_map/rnm,nk->rmk/dot_general | solution.py:38
  542.0 94.5 %all_to_all.117 = f32[2,128,4096]{1,0,2:T(2,128)S(1)} all-to-all(f32[2,128,4096]{1,0,2:T(2,128)S(1)} %pad_maximum_fusion.2), channel_id=1, replica_groups=mesh['rows'=8,'cols'=4] {'cols'}, dimensions={2} | all-to-all | bytes 8388608 | tf_op jit(solution)/shard_map/all_to_all | solution.py:66
  651.5 54.8 %all_to_all.118 = f32[2,1024,512]{2,0,1:T(2,128)S(1)} all-to-all(f32[2,1024,512]{2,0,1:T(2,128)} %copy.187), channel_id=1, replica_groups=mesh['rows'=8,'cols'=4] {'rows'}, dimensions={1} | all-to-all | bytes 8388608 | tf_op jit(solution)/shard_map/all_to_all | solution.py:68
  713.5 10.3 %fusion.54 = f32[128,8,512]{2,0,1:T(8,128)} fusion(f32[128,512,8]{1,0,2:T(8,128)} %copy.190), kind=kOutput, calls=%fused_computation.80 | convolution fusion | flops 3224895488 | bytes 4194304 | tf_op jit(solution)/shard_map/rnm,nk->rmk/dot_general | solution.py:38
  723.8 8.4 fusion.66
  736.0 9.9 %convolution_subtract_fusion = f32[128,8,512]{2,0,1:T(8,128)S(1)} fusion(f32[128,8,512]{2,0,1:T(8,128)} %fusion.66, f32[128,512,8]{1,0,2:T(8,128)S(1)} %copy.192), kind=kOutput, calls=%fused_computation.69 | convolution fusion | flops 3225419776 | bytes 6291456 | tf_op jit(solution)/shard_map/rnm,nk->rmk/dot_general | solution.py:38
  745.9 9.2 %multiply_subtract_fusion = (f32[128,8,512]{2,0,1:T(8,128)S(1)}, f32[128,8,512]{2,0,1:T(8,128)S(1)}) fusion(f32[128,8,512]{2,0,1:T(8,128)S(1)} %convolution_subtract_fusion, f32[8,512]{1,0:T(8,128)S(1)} %get-tuple-element.32, f32[8,512]{1,0:T(8,128)S(1)} %get-tuple-element.33, f32[128,8,512]{2,0,1:T(8,128)S(1)} %copy-done.7, f32[128,512,8]{1,0,2:T(8,128)S(1)} %copy.192), kind=kOutput, calls=%fused_computation.29 | convolution fusion | flops 3228565504 | bytes 10518528 | tf_op jit(solution)/shard_map/rnm,nk->rmk/dot_general | solution.py:38
  784.5 7.5 multiply_reduce_fusion
  792.0 41.6 %all-to-all-done.7 = f32[2,128,4096]{1,0,2:T(2,128)} async-done(((f32[2,128,4096]{1,0,2:T(2,128)}), f32[2,128,4096]{1,0,2:T(2,128)}, u32[]{:S(2)}, u32[]{:S(2)}) %all-to-all-start.7) | async-done | bytes 4194336 | tf_op jit(solution)/shard_map/all_to_all | solution.py:76
  854.6 38.0 %all-reduce = (f32[16]{0:T(128)S(1)}, f32[]{:T(128)}) all-reduce(f32[16]{0:T(128)S(1)} %multiply_reduce_fusion, f32[]{:T(128)S(6)} %add.265), channel_id=1, replica_groups=mesh['rows'=8,'cols'=4] {'rows','cols'}, use_global_device_ids=true, to_apply=%region_0.1 | all-reduce | flops 17 | bytes 136 | tf_op jit(solution)/shard_map/psum | solution.py:103
  (109 shorter events, 209.3 us)
Async XLA Ops:
  3.9 4.5 copy-start.16
  4.0 4.5 copy-start.14
  17.9 99.9 %all-to-all-start = ((f32[2,512,1024]{2,0,1:T(2,128)}), f32[2,512,1024]{2,0,1:T(2,128)}, u32[]{:S(2)}, u32[]{:S(2)}) async-start(f32[2,512,1024]{2,0,1:T(2,128)} %pad_maximum_fusion), calls=%async_computation | async-start | bytes 8388608 | tf_op jit(solution)/shard_map/all_to_all | solution.py:72
  127.4 10.3 %copy-start.10 = (f32[128,512,8]{1,0,2:T(8,128)S(1)}, f32[128,512,8]{1,0,2:T(8,128)}, u32[]{:S(2)}) copy-start(f32[128,512,8]{1,0,2:T(8,128)} %copy.151) | copy-start | bytes 6291460
  137.6 8.4 copy-start.3
  149.8 10.0 %copy-start.8 = (f32[128,8,512]{2,0,1:T(8,128)S(1)}, f32[128,8,512]{2,0,1:T(8,128)}, u32[]{:S(2)}) copy-start(f32[128,8,512]{2,0,1:T(8,128)} %fusion.62) | copy-start | bytes 6291460
  362.6 10.3 %copy-start.11 = (f32[128,512,8]{1,0,2:T(8,128)S(1)}, f32[128,512,8]{1,0,2:T(8,128)}, u32[]{:S(2)}) copy-start(f32[128,512,8]{1,0,2:T(8,128)} %copy.167) | copy-start | bytes 6291460
  372.9 8.4 copy-start.4
  385.0 10.0 %copy-start.9 = (f32[128,8,512]{2,0,1:T(8,128)S(1)}, f32[128,8,512]{2,0,1:T(8,128)}, u32[]{:S(2)}) copy-start(f32[128,8,512]{2,0,1:T(8,128)} %fusion.59) | copy-start | bytes 6291460
  411.8 3.9 copy-start.18
  411.8 30.5 %all-to-all-start.3 = ((f32[1,128,4096]{1,0,2:T(1,128)}), f32[1,128,4096]{1,0,2:T(1,128)S(1)}, u32[]{:S(2)}, u32[]{:S(2)}) async-start(f32[1,128,4096]{1,0,2:T(1,128)} %bitcast.209), calls=%async_computation.3 | async-start | bytes 4194304 | tf_op jit(solution)/shard_map/all_to_all | solution.py:76
  442.3 2.1 copy-start.6
  442.3 2.2 copy-start.13
  447.6 1.4 copy-start
  713.5 10.3 %copy-start.12 = (f32[128,512,8]{1,0,2:T(8,128)S(1)}, f32[128,512,8]{1,0,2:T(8,128)}, u32[]{:S(2)}) copy-start(f32[128,512,8]{1,0,2:T(8,128)} %copy.190) | copy-start | bytes 6291460
  723.8 8.4 copy-start.5
  736.0 10.0 %copy-start.7 = (f32[128,8,512]{2,0,1:T(8,128)S(1)}, f32[128,8,512]{2,0,1:T(8,128)}, u32[]{:S(2)}) copy-start(f32[128,8,512]{2,0,1:T(8,128)} %fusion.54) | copy-start | bytes 6291460
  779.8 4.7 copy-start.1
  779.8 53.8 %all-to-all-start.7 = ((f32[2,128,4096]{1,0,2:T(2,128)}), f32[2,128,4096]{1,0,2:T(2,128)}, u32[]{:S(2)}, u32[]{:S(2)}) async-start(f32[2,128,4096]{1,0,2:T(2,128)} %pad_maximum_fusion.3), calls=%async_computation.7 | async-start | bytes 8388608 | tf_op jit(solution)/shard_map/all_to_all | solution.py:76
  842.0 5.0 copy-start.2
  842.0 5.0 copy-start.15
  842.0 5.0 copy-start.17
where the time goes:
time: 906 us; the launch traced here: 897 us
  blocking collectives  384 us (42%)
  matrix products  198 us (22%)
  waiting for transfers between devices  139 us (15%)
  local copies, waits for them, and re-layouts  102 us (11%)
  other arithmetic  51.1 us (6%)
  starting transfers between devices  15.1 us (2%)
    all_to_all x2, blocking collectives, middle_step(): lax.all_to_all(spread, 'cols', split_axis=2, concat_axis=1, tiled=True)  190 us
    dot_general x14, matrix products, apply_big(): return jnp.einsum('rnm,nk->rmk', block, table, precision=highest)  131 us
    all_to_all x2, blocking collectives, middle_step(): lax.all_to_all(flipped, 'rows', split_axis=1, concat_axis=2, tiled=True)  108 us
    all_to_all x1, waiting for transfers between devices, grid_transform(): lax.all_to_all(pieces, 'cols', split_axis=1, concat_axis=2, tiled=True)  93.3 us
    all_to_all x1, blocking collectives, grid_transform(): lax.all_to_all(pieces, 'cols', split_axis=1, concat_axis=2, tiled=True)  48.1 us
    all_to_all x2, waiting for transfers between devices, grid_transform(): lax.all_to_all(second, 'rows', split_axis=2, concat_axis=1, tiled=True)  45.5 us
    dot_general x14, matrix products, apply_small(): return jnp.einsum('rmk,mj->rjk', block, table, precision=highest)  44.6 us
    psum x1, blocking collectives, shards(): lax.psum((partial_coef, partial_loss), ('rows', 'cols'))  38 us
  transfers between devices with their start and end apart: 3, of which 3 were waited for; matrix products, arithmetic and copies ran while one was open for 3% of the time, Pallas kernels for 0%

commit v1 on v0

--- a/solution.py
+++ b/solution.py
@@ -7,6 +7,18 @@
 NG = 4096
 lasso_weight = 0.02
 ridge_weight = 0.1
+
+
+def in_blocks(x, dim, devices):
+    dims = x.shape
+    blocks = x.reshape(*dims[:dim], devices, dims[dim] // devices, *dims[dim + 1 :])
+    return jnp.moveaxis(blocks, dim, 0)
+
+
+def joined_along(pieces, dim):
+    pieces = jnp.moveaxis(pieces, 0, dim)
+    shape = pieces.shape
+    return pieces.reshape(*shape[:dim], shape[dim] * shape[dim + 1], *shape[dim + 2 :])
 
 
 def field_spectrum(field_hyper, wave_row, wave_col):
@@ -69,7 +81,15 @@
 
 
 def grid_transform(pieces, want_real):
-    full_rows = lax.all_to_all(pieces, "cols", split_axis=1, concat_axis=2, tiled=True)
+    count, index = (lax.axis_size("cols"), lax.axis_index("cols"))
+    blocks = in_blocks(pieces, 1, count)
+    out = blocks
+    for hop in range(1, count):
+        target, source = ((index + hop) % count, (index - hop) % count)
+        sent = lax.dynamic_index_in_dim(blocks, target, 0)
+        received = lax.ppermute(sent, "cols", [(i, (i + hop) % count) for i in range(count)])
+        out = lax.dynamic_update_slice_in_dim(out, received, source, axis=0)
+    full_rows = joined_along(out, 2)
     halfway = inverse_transform(full_rows, False)
     columns = middle_step(halfway)
     second = inverse_transform(columns, want_real)

time: 906 us -> 907 us (level)
  waiting for transfers between devices: 139 us -> 94.2 us
  blocking collectives: 384 us -> 421 us
  matrix products: 198 us -> 215 us
    all_to_all x1 -> x0, waiting for transfers between devices: 93.3 us -> none  [grid_transform(): lax.all_to_all(pieces, 'cols', split_axis=1, concat_axis=2, tiled=True)]
    ppermute x0 -> x6, waiting for transfers between devices: none -> 90.3 us  [grid_transform(): lax.ppermute(sent, 'cols', [(i, (i + hop) % count) for i in range(count)])]
    all_to_all x2 -> x1, waiting for transfers between devices: 45.5 us -> 3.89 us  [grid_transform(): lax.all_to_all(second, 'rows', split_axis=2, concat_axis=1, tiled=True)]
    all_to_all x2, blocking collectives: 190 us -> 223 us  [middle_step(): lax.all_to_all(spread, 'cols', split_axis=2, concat_axis=1, tiled=True)]
    dot_general x14, matrix products: 44.6 us -> 57 us  [apply_small(): return jnp.einsum('rmk,mj->rjk', block, table, precision=highest)]
    another operation x2 -> x0, other arithmetic: 9.58 us -> none  [shards(): scaled = jnp.stack([spectrum * white_real, spectrum * white_imag])]
  transfers between devices with their start and end apart: 3 -> 7, of which waited for: 3 -> 6; matrix products, arithmetic and copies ran while one was open for 3% -> 4% of each run, Pallas kernels for 0% -> 0%
where the time goes in v1:
time: 907 us; the launch traced here: 903 us
  blocking collectives  421 us (46%)
  matrix products  215 us (24%)
  local copies, waits for them, and re-layouts  106 us (12%)
  waiting for transfers between devices  94.2 us (10%)
  other arithmetic  46.6 us (5%)
  starting transfers between devices  12 us (1%)
    all_to_all x2, blocking collectives, middle_step(): lax.all_to_all(spread, 'cols', split_axis=2, concat_axis=1, tiled=True)  223 us
    dot_general x14, matrix products, apply_big(): return jnp.einsum('rnm,nk->rmk', block, table, precision=highest)  135 us
    all_to_all x2, blocking collectives, middle_step(): lax.all_to_all(flipped, 'rows', split_axis=1, concat_axis=2, tiled=True)  108 us
    ppermute x6, waiting for transfers between devices, grid_transform(): lax.ppermute(sent, 'cols', [(i, (i + hop) % count) for i in range(count)])  90.3 us
    dot_general x14, matrix products, apply_small(): return jnp.einsum('rmk,mj->rjk', block, table, precision=highest)  57 us
    all_to_all x1, blocking collectives, grid_transform(): lax.all_to_all(second, 'rows', split_axis=2, concat_axis=1, tiled=True)  51.6 us
    psum x1, blocking collectives, shards(): lax.psum((partial_coef, partial_loss), ('rows', 'cols'))  37.9 us
    dot_general x1, matrix products, shards(): linear = jnp.einsum('j,jrc->rc', coefficients, cov_full, precision=highest)  22.7 us
  transfers between devices with their start and end apart: 7, of which 6 were waited for; matrix products, arithmetic and copies ran while one was open for 4% of the time, Pallas kernels for 0%

profile of v1, /device:TPU:0, one launch (start us, length us, event | category | flops | bytes accessed | tf_op | source)
XLA Modules:
  0.0 902.9 jit_solution(6545684004581918749)
XLA Ops:
  20.4 19.9 %collective-permute-done = f32[1,2,128,1024]{3,2,0,1:T(8,128)} collective-permute-done((f32[1,2,128,1024]{3,2,0,1:T(8,128)}, f32[1,2,128,1024]{3,2,0,1:T(8,128)}, u32[]{:S(2)}, u32[]{:S(2)}) %collective-permute-start) | collective-permute-done | bytes 1048608 | tf_op jit(solution)/shard_map/ppermute | solution.py:90
  41.6 42.8 %collective-permute-done.1 = f32[1,2,128,1024]{3,2,0,1:T(8,128)} collective-permute-done((f32[1,2,128,1024]{3,2,0,1:T(8,128)}, f32[1,2,128,1024]{3,2,0,1:T(8,128)}, u32[]{:S(2)}, u32[]{:S(2)}) %collective-permute-start.1) | collective-permute-done | bytes 1048608 | tf_op jit(solution)/shard_map/ppermute | solution.py:90
  91.9 10.3 %fusion.80 = f32[128,8,512]{2,0,1:T(8,128)} fusion(f32[128,512,8]{1,0,2:T(8,128)} %copy.147), kind=kOutput, calls=%fused_computation.112 | convolution fusion | flops 3224895488 | bytes 4194304 | tf_op jit(solution)/shard_map/rnm,nk->rmk/dot_general | solution.py:50
  102.2 8.4 fusion.68
  114.4 10.6 %convolution_subtract_fusion.2 = f32[128,8,512]{2,0,1:T(8,128)S(1)} fusion(f32[128,8,512]{2,0,1:T(8,128)} %fusion.80, f32[128,512,8]{1,0,2:T(8,128)S(1)} %copy.149), kind=kOutput, calls=%fused_computation.79 | convolution fusion | flops 3225419776 | bytes 6291456 | tf_op jit(solution)/shard_map/rnm,nk->rmk/dot_general | solution.py:50
  125.1 10.5 %multiply_subtract_fusion.3 = (f32[128,8,512]{2,0,1:T(8,128)S(1)}, f32[128,8,512]{2,0,1:T(8,128)S(1)}) fusion(f32[128,8,512]{2,0,1:T(8,128)S(1)} %convolution_subtract_fusion.2, f32[8,512]{1,0:T(8,128)S(1)} %get-tuple-element.38, f32[8,512]{1,0:T(8,128)S(1)} %get-tuple-element.39, f32[128,8,512]{2,0,1:T(8,128)S(1)} %copy-done.11, f32[128,512,8]{1,0,2:T(8,128)} %copy-done.1), kind=kOutput, calls=%fused_computation.48 | convolution fusion | flops 3228565504 | bytes 10518528 | tf_op jit(solution)/shard_map/rnm,nk->rmk/dot_general | solution.py:50
  164.0 117.3 %all_to_all.84 = f32[2,128,4096]{1,0,2:T(2,128)S(1)} all-to-all(f32[2,128,4096]{1,0,2:T(2,128)S(1)} %pad_maximum_fusion.1), channel_id=1, replica_groups=mesh['rows'=8,'cols'=4] {'cols'}, dimensions={2} | all-to-all | bytes 8388608 | tf_op jit(solution)/shard_map/all_to_all | solution.py:78
  296.3 53.3 %all_to_all.85 = f32[2,1024,512]{2,0,1:T(2,128)S(1)} all-to-all(f32[2,1024,512]{2,0,1:T(2,128)} %copy.160), channel_id=1, replica_groups=mesh['rows'=8,'cols'=4] {'rows'}, dimensions={1} | all-to-all | bytes 8388608 | tf_op jit(solution)/shard_map/all_to_all | solution.py:80
  356.8 10.3 %fusion.77 = f32[128,8,512]{2,0,1:T(8,128)} fusion(f32[128,512,8]{1,0,2:T(8,128)} %copy.163), kind=kOutput, calls=%fused_computation.109 | convolution fusion | flops 3224895488 | bytes 4194304 | tf_op jit(solution)/shard_map/rnm,nk->rmk/dot_general | solution.py:50
  367.1 8.4 fusion.65
  379.3 9.9 %convolution_subtract_fusion.1 = f32[128,8,512]{2,0,1:T(8,128)S(1)} fusion(f32[128,8,512]{2,0,1:T(8,128)} %fusion.77, f32[128,512,8]{1,0,2:T(8,128)S(1)} %copy.165), kind=kOutput, calls=%fused_computation.77 | convolution fusion | flops 3225419776 | bytes 6291456 | tf_op jit(solution)/shard_map/rnm,nk->rmk/dot_general | solution.py:50
  389.2 8.8 multiply_subtract_fusion.2
  409.8 22.7 %fusion = f32[1,512,1024]{2,0,1:T(1,128)} fusion(bf16[16,512,1024]{2,1,0:T(8,128)(2,1)} %param.9, f32[16]{0:T(128)S(1)} %copy-done.21), kind=kOutput, calls=%fused_computation.1 | convolution fusion | flops 100663296 | bytes 18874432 | tf_op jit(solution)/shard_map/j,jrc->rc/dot_general | solution.py:112
  461.7 20.0 %collective-permute-done.4 = f32[1,1,128,1024]{3,2,0,1:T(8,128)S(1)} collective-permute-done((f32[1,1,128,1024]{3,2,0,1:T(8,128)S(1)}, f32[1,1,128,1024]{3,2,0,1:T(8,128)S(1)}, u32[]{:S(2)}, u32[]{:S(2)}) %collective-permute-start.4) | collective-permute-done | bytes 524320 | tf_op jit(solution)/shard_map/ppermute | solution.py:90
  487.3 8.4 fusion.74
  495.7 10.5 %multiply_subtract_fusion.1 = (f32[128,8,512]{2,0,1:T(8,128)S(1)}, f32[128,8,512]{2,0,1:T(8,128)S(1)}) fusion(f32[128,8,512]{2,0,1:T(8,128)S(1)} %fusion.74, f32[8,512]{1,0:T(8,128)S(1)} %get-tuple-element.38, f32[8,512]{1,0:T(8,128)S(1)} %get-tuple-element.39, f32[128,512,8]{1,0,2:T(8,128)} %copy-done.13), kind=kOutput, calls=%fused_computation.40 | convolution fusion | flops 3228041216 | bytes 8421376 | tf_op jit(solution)/shard_map/rnm,nk->rmk/dot_general | solution.py:50
  534.3 105.7 %all_to_all.86 = f32[2,128,4096]{1,0,2:T(2,128)S(1)} all-to-all(f32[2,128,4096]{1,0,2:T(2,128)S(1)} %pad_maximum_fusion.2), channel_id=1, replica_groups=mesh['rows'=8,'cols'=4] {'cols'}, dimensions={2} | all-to-all | bytes 8388608 | tf_op jit(solution)/shard_map/all_to_all | solution.py:78
  655.0 55.1 %all_to_all.87 = f32[2,1024,512]{2,0,1:T(2,128)S(1)} all-to-all(f32[2,1024,512]{2,0,1:T(2,128)} %copy.183), channel_id=1, replica_groups=mesh['rows'=8,'cols'=4] {'rows'}, dimensions={1} | all-to-all | bytes 8388608 | tf_op jit(solution)/shard_map/all_to_all | solution.py:80
  717.3 10.3 %fusion.72 = f32[128,8,512]{2,0,1:T(8,128)} fusion(f32[128,512,8]{1,0,2:T(8,128)} %copy.186), kind=kOutput, calls=%fused_computation.104 | convolution fusion | flops 3224895488 | bytes 4194304 | tf_op jit(solution)/shard_map/rnm,nk->rmk/dot_general | solution.py:50
  727.6 8.4 fusion.60
  741.1 9.9 %convolution_subtract_fusion = f32[128,8,512]{2,0,1:T(8,128)S(1)} fusion(f32[128,8,512]{2,0,1:T(8,128)} %fusion.72, f32[128,512,8]{1,0,2:T(8,128)S(1)} %copy.188), kind=kOutput, calls=%fused_computation.75 | convolution fusion | flops 3225419776 | bytes 6291456 | tf_op jit(solution)/shard_map/rnm,nk->rmk/dot_general | solution.py:50
  751.0 10.7 %multiply_subtract_fusion = (f32[128,8,512]{2,0,1:T(8,128)S(1)}, f32[128,8,512]{2,0,1:T(8,128)S(1)}) fusion(f32[128,8,512]{2,0,1:T(8,128)S(1)} %convolution_subtract_fusion, f32[8,512]{1,0:T(8,128)S(1)} %get-tuple-element.38, f32[8,512]{1,0:T(8,128)S(1)} %get-tuple-element.39, f32[128,8,512]{2,0,1:T(8,128)S(1)} %copy-done.10, f32[128,512,8]{1,0,2:T(8,128)} %copy-done), kind=kOutput, calls=%fused_computation.36 | convolution fusion | flops 3228565504 | bytes 10518528 | tf_op jit(solution)/shard_map/rnm,nk->rmk/dot_general | solution.py:50
  790.1 51.6 %all_to_all.88 = f32[2,128,4096]{1,0,2:T(2,128)S(1)} all-to-all(f32[2,128,4096]{1,0,2:T(2,128)S(1)} %pad_maximum_fusion.3), channel_id=1, replica_groups=mesh['rows'=8,'cols'=4] {'rows'}, dimensions={2} | all-to-all | bytes 8388608 | tf_op jit(solution)/shard_map/all_to_all | solution.py:96
  860.5 37.9 %all-reduce = (f32[16]{0:T(128)S(1)}, f32[]{:T(128)}) all-reduce(f32[16]{0:T(128)S(1)} %multiply_reduce_fusion, f32[]{:T(128)S(6)} %add.346), channel_id=1, replica_groups=mesh['rows'=8,'cols'=4] {'rows','cols'}, use_global_device_ids=true, to_apply=%region_0.1 | all-reduce | flops 17 | bytes 136 | tf_op jit(solution)/shard_map/psum | solution.py:123
  (128 shorter events, 232.8 us)
Async XLA Ops:
  0.7 7.8 copy-start.17
  4.0 4.5 copy-start.19
  10.9 29.5 %collective-permute-start = (f32[1,2,128,1024]{3,2,0,1:T(8,128)}, f32[1,2,128,1024]{3,2,0,1:T(8,128)}, u32[]{:S(2)}, u32[]{:S(2)}) collective-permute-start(f32[1,2,128,1024]{3,2,0,1:T(8,128)} %get-tuple-element.28), channel_id=1, source_target_pairs={{0,1},{1,2},{2,3},{3,0},{4,5},{5,6},{6,7},{7,4},{8,9},{9,10},{10,1... | collective-permute-start | bytes 3145736 | tf_op jit(solution)/shard_map/ppermute | solution.py:90
  13.9 70.6 %collective-permute-start.1 = (f32[1,2,128,1024]{3,2,0,1:T(8,128)}, f32[1,2,128,1024]{3,2,0,1:T(8,128)}, u32[]{:S(2)}, u32[]{:S(2)}) collective-permute-start(f32[1,2,128,1024]{3,2,0,1:T(8,128)} %get-tuple-element.29), channel_id=1, source_target_pairs={{0,2},{1,3},{2,0},{3,1},{4,6},{5,7},{6,4},{7,5},{8,10},{9,11},{10,... | collective-permute-start | bytes 3145736 | tf_op jit(solution)/shard_map/ppermute | solution.py:90
  16.5 69.3 %collective-permute-start.2 = (f32[1,2,128,1024]{3,2,0,1:T(8,128)}, f32[1,2,128,1024]{3,2,0,1:T(8,128)S(1)}, u32[]{:S(2)}, u32[]{:S(2)}) collective-permute-start(f32[1,2,128,1024]{3,2,0,1:T(8,128)} %get-tuple-element.27), channel_id=1, source_target_pairs={{0,3},{1,0},{2,1},{3,2},{4,7},{5,4},{6,5},{7,6},{8,11},{9,8},{10,9... | collective-permute-start | bytes 3145736 | tf_op jit(solution)/shard_map/ppermute | solution.py:90
  91.9 10.3 %copy-start.14 = (f32[128,512,8]{1,0,2:T(8,128)S(1)}, f32[128,512,8]{1,0,2:T(8,128)}, u32[]{:S(2)}) copy-start(f32[128,512,8]{1,0,2:T(8,128)} %copy.147) | copy-start | bytes 6291460
  102.2 8.4 copy-start.4
  114.4 10.7 %copy-start.1 = (f32[128,512,8]{1,0,2:T(8,128)}, f32[128,512,8]{1,0,2:T(8,128)S(1)}, u32[]{:S(2)}) copy-start(f32[128,512,8]{1,0,2:T(8,128)S(1)} %copy.149) | copy-start | bytes 6291460
  114.4 10.7 %copy-start.11 = (f32[128,8,512]{2,0,1:T(8,128)S(1)}, f32[128,8,512]{2,0,1:T(8,128)}, u32[]{:S(2)}) copy-start(f32[128,8,512]{2,0,1:T(8,128)} %fusion.68) | copy-start | bytes 6291460
  155.9 3.1 copy-start.7
  356.8 10.3 %copy-start.15 = (f32[128,512,8]{1,0,2:T(8,128)S(1)}, f32[128,512,8]{1,0,2:T(8,128)}, u32[]{:S(2)}) copy-start(f32[128,512,8]{1,0,2:T(8,128)} %copy.163) | copy-start | bytes 6291460
  367.1 8.4 copy-start.5
  379.3 9.9 %copy-start.12 = (f32[128,8,512]{2,0,1:T(8,128)S(1)}, f32[128,8,512]{2,0,1:T(8,128)}, u32[]{:S(2)}) copy-start(f32[128,8,512]{2,0,1:T(8,128)} %fusion.65) | copy-start | bytes 6291460
  405.6 4.2 copy-start.21
  405.6 30.7 %all-to-all-start.2 = ((f32[1,128,4096]{1,0,2:T(1,128)}), f32[1,128,4096]{1,0,2:T(1,128)S(1)}, u32[]{:S(2)}, u32[]{:S(2)}) async-start(f32[1,128,4096]{1,0,2:T(1,128)} %bitcast.215), calls=%async_computation.2 | async-start | bytes 4194304 | tf_op jit(solution)/shard_map/all_to_all | solution.py:96
  446.5 14.9 %collective-permute-start.3 = (f32[1,1,128,1024]{3,2,0,1:T(8,128)S(1)}, f32[1,1,128,1024]{3,2,0,1:T(8,128)S(1)}, u32[]{:S(2)}, u32[]{:S(2)}) collective-permute-start(f32[1,1,128,1024]{3,2,0,1:T(8,128)S(1)} %constant_dynamic-slice_fusion.2), channel_id=1, source_target_pairs={{0,1},{1,2},{2,3},{3,0},{4,5},{5,6},{6,7},{7,4},{8,9},{9,10},{10,1... | collective-permute-start | bytes 1572872 | tf_op jit(solution)/shard_map/ppermute | solution.py:90
  461.6 20.2 %collective-permute-start.4 = (f32[1,1,128,1024]{3,2,0,1:T(8,128)S(1)}, f32[1,1,128,1024]{3,2,0,1:T(8,128)S(1)}, u32[]{:S(2)}, u32[]{:S(2)}) collective-permute-start(f32[1,1,128,1024]{3,2,0,1:T(8,128)S(1)} %get-tuple-element.31), channel_id=1, source_target_pairs={{0,2},{1,3},{2,0},{3,1},{4,6},{5,7},{6,4},{7,5},{8,10},{9,11},{10,... | collective-permute-start | bytes 1572872 | tf_op jit(solution)/shard_map/ppermute | solution.py:90
  461.7 20.5 %collective-permute-start.5 = (f32[1,1,128,1024]{3,2,0,1:T(8,128)S(1)}, f32[1,1,128,1024]{3,2,0,1:T(8,128)S(1)}, u32[]{:S(2)}, u32[]{:S(2)}) collective-permute-start(f32[1,1,128,1024]{3,2,0,1:T(8,128)S(1)} %get-tuple-element.30), channel_id=1, source_target_pairs={{0,3},{1,0},{2,1},{3,2},{4,7},{5,4},{6,5},{7,6},{8,11},{9,8},{10,9... | collective-permute-start | bytes 1572872 | tf_op jit(solution)/shard_map/ppermute | solution.py:90
  717.3 10.3 %copy-start.16 = (f32[128,512,8]{1,0,2:T(8,128)S(1)}, f32[128,512,8]{1,0,2:T(8,128)}, u32[]{:S(2)}) copy-start(f32[128,512,8]{1,0,2:T(8,128)} %copy.186) | copy-start | bytes 6291460
  727.6 8.4 copy-start.6
  741.1 9.9 %copy-start.10 = (f32[128,8,512]{2,0,1:T(8,128)S(1)}, f32[128,8,512]{2,0,1:T(8,128)}, u32[]{:S(2)}) copy-start(f32[128,8,512]{2,0,1:T(8,128)} %fusion.60) | copy-start | bytes 6291460
  847.9 5.0 copy-start.3
  847.9 5.0 copy-start.18
  847.9 5.0 copy-start.20
  (5 other events, 11.2 us)
